TPU v7x, 512 devices: a whole 4x4x16 slice. The times are simulated.
512 devices in a mesh: row: 32 (over x, z_lo, core), col: 16 (over y, z_hi).
Axes of the slice: x: 4, y: 4, z: 16 (z_hi: 4, z_lo: 4; z = z_hi * 4 + z_lo), core: 2. Of those that a mesh axis runs over, the one named last changes fastest.
Arguments:
- amplitudes: bfloat16 [2, 2048, 2048], P(None, 'row', 'col'), may hold values from -6 to 6
- factor: bfloat16 [2048, 4096], P('row', 'col'), may hold values from -0.125 to 0.125
- kernel: float32 [4096, 4096], P('row', 'col'), may hold values from -6 to 6
Outputs:
- ladder: bfloat16 [2, 2048, 2048], P(None, 'row', 'col')
All inputs are finite; a program needn't handle non-finite values.
Results may differ from a plain program's by a relative error of at most 0.015.
Values may be sent and summed in bfloat16 or wider, within the bound.
A program may use at most 64 MiB of HBM per device.

v0:
```python
import jax
import jax.numpy as jnp
from jax import lax
from jax.sharding import PartitionSpec as P


def in_order(parts, dim):
    parts = jnp.moveaxis(parts, 0, dim)
    shape = parts.shape
    return parts.reshape(*shape[:dim], shape[dim] * shape[dim + 1], *shape[dim + 2 :])


def sent_to_all(value, axis):
    copies = jnp.broadcast_to(value, (lax.axis_size(axis), *value.shape))
    return lax.all_to_all(copies, axis, split_axis=0, concat_axis=0, tiled=True)


def gathered_copies(value, axis, dim):
    return in_order(sent_to_all(value, axis), dim)


def cut_along(value, dim, size):
    shape = value.shape
    parts = value.reshape(*shape[:dim], size, shape[dim] // size, *shape[dim + 1 :])
    return jnp.moveaxis(parts, dim, 0)


def sent_and_summed(value, axis, dim):
    size = lax.axis_size(axis)
    parts = lax.all_to_all(cut_along(value, dim, size), axis, 0, 0, tiled=True)
    return jnp.sum(parts.astype(jnp.float32), axis=0)


def per_device(amplitudes, factor, kernel):
    factor_cols = gathered_copies(factor, "row", 0)
    factor_rows = gathered_copies(factor, "col", 1)
    factor_first = lax.all_to_all(factor_rows, "row", split_axis=1, concat_axis=0, tiled=True)
    factor_part = factor_cols
    projected = jnp.einsum(
        "pak,kq->paq",
        gathered_copies(amplitudes, "col", 2),
        factor_part,
        preferred_element_type=jnp.float32,
    ).astype(jnp.bfloat16)
    factor_part = factor_first
    grid_pairs = jnp.einsum(
        "kp,nkq->npq",
        factor_part,
        gathered_copies(projected, "row", 1),
        preferred_element_type=jnp.float32,
    )
    scaled = (kernel[None] * grid_pairs).astype(jnp.bfloat16)
    factor_part = factor_cols
    half_back = sent_and_summed(
        jnp.einsum("bq,npq->bnp", factor_part, scaled, preferred_element_type=jnp.float32).astype(
            jnp.bfloat16
        ),
        "col",
        0,
    )
    half_back = half_back.astype(jnp.bfloat16)
    factor_part = factor_rows
    result = jnp.einsum(
        "ak,bnk->nab",
        factor_part,
        gathered_copies(half_back, "row", 2),
        preferred_element_type=jnp.float32,
    )
    return result.astype(jnp.bfloat16)


def solution(mesh):
    placed = (P(None, "row", "col"), P("row", "col"), P("row", "col"))
    return jax.shard_map(
        per_device, mesh=mesh, in_specs=placed, out_specs=P(None, "row", "col"), check_vma=False
    )
```

profile of v0, /device:TPU:1, one launch (start us, length us, event | category | flops | bytes accessed | tf_op | source)
XLA Modules:
  0.0 323.4 jit_solution(5627007424775163365)
XLA Ops:
  0.0 0.0 copy-start.3
  0.0 0.9 broadcast_in_dim.16
  0.9 45.3 %all_to_all.46 = bf16[16,2,64,128]{3,2,1,0:T(8,128)(2,1)S(1)} all-to-all(bf16[16,2,64,128]{3,2,1,0:T(8,128)(2,1)S(1)} %broadcast_in_dim.16), channel_id=1, replica_groups=mesh['row'=32,'col'=16] {'col'}, dimensions={0} | all-to-all | bytes 1048576 | tf_op jit(solution)/shard_map/all_to_all | solution.py:15
  46.2 0.8 broadcast_in_dim.19
  47.0 29.1 %all_to_all.47 = bf16[16,64,256]{2,1,0:T(8,128)(2,1)S(1)} all-to-all(bf16[16,64,256]{2,1,0:T(8,128)(2,1)S(1)} %broadcast_in_dim.19), channel_id=1, replica_groups=mesh['row'=32,'col'=16] {'col'}, dimensions={0} | all-to-all | bytes 1048576 | tf_op jit(solution)/shard_map/all_to_all | solution.py:15
  76.1 0.0 copy-done.3
  76.1 1.1 broadcast_in_dim.17
  77.2 21.4 %all-to-all-start.1 = ((bf16[32,64,256]{2,1,0:T(8,128)(2,1)}), bf16[32,64,256]{2,1,0:T(8,128)(2,1)S(1)}, u32[]{:S(2)}, u32[]{:S(2)}) async-start(bf16[32,64,256]{2,1,0:T(8,128)(2,1)} %broadcast_in_dim.17), calls=%async_computation.1 | async-start | bytes 2097152 | tf_op jit(solution)/shard_map/all_to_all | solution.py:15
  98.6 0.3 copy.14
  98.9 0.0 copy-start
  98.9 0.2 all_to_all.34
  99.1 1.0 copy.15
  100.1 26.3 %all-to-all-done.1 = bf16[32,64,256]{2,1,0:T(8,128)(2,1)S(1)} async-done(((bf16[32,64,256]{2,1,0:T(8,128)(2,1)}), bf16[32,64,256]{2,1,0:T(8,128)(2,1)S(1)}, u32[]{:S(2)}, u32[]{:S(2)}) %all-to-all-start.1) | async-done | bytes 1048608 | tf_op jit(solution)/shard_map/all_to_all | solution.py:15
  126.4 3.9 %all-to-all-start.4 = ((bf16[64,32,128]{2,0,1:T(8,128)(2,1)}), bf16[64,32,128]{2,0,1:T(8,128)(2,1)S(1)}, u32[]{:S(2)}, u32[]{:S(2)}) async-start(bf16[64,32,128]{2,0,1:T(8,128)(2,1)} %copy.15), calls=%async_computation.4 | async-start | bytes 1048576 | tf_op jit(solution)/shard_map/all_to_all | solution.py:37
  130.3 0.3 convolution_convert_fusion.1
  130.6 0.0 copy-done
  130.6 16.5 %all-to-all-done.4 = bf16[64,32,128]{2,0,1:T(8,128)(2,1)S(1)} async-done(((bf16[64,32,128]{2,0,1:T(8,128)(2,1)}), bf16[64,32,128]{2,0,1:T(8,128)(2,1)S(1)}, u32[]{:S(2)}, u32[]{:S(2)}) %all-to-all-start.4) | async-done | bytes 524320 | tf_op jit(solution)/shard_map/all_to_all | solution.py:37
  147.1 0.0 copy-start.2
  147.1 1.6 broadcast_in_dim.18
  148.7 0.0 copy-start.4
  148.7 0.0 copy-done.2
  148.7 3.9 %all-to-all-start.2 = ((bf16[32,2,64,256]{3,2,1,0:T(8,128)(2,1)}), bf16[32,2,64,256]{3,2,1,0:T(8,128)(2,1)S(1)}, u32[]{:S(2)}, u32[]{:S(2)}) async-start(bf16[32,2,64,256]{3,2,1,0:T(8,128)(2,1)} %broadcast_in_dim.18), calls=%async_computation.2 | async-start | bytes 4194304 | tf_op jit(solution)/shard_map/all_to_all | solution.py:15
  152.6 0.0 copy-done.4
  152.6 0.1 copy.12
  152.7 49.8 %all-to-all-done.2 = bf16[32,2,64,256]{3,2,1,0:T(8,128)(2,1)S(1)} async-done(((bf16[32,2,64,256]{3,2,1,0:T(8,128)(2,1)}), bf16[32,2,64,256]{3,2,1,0:T(8,128)(2,1)S(1)}, u32[]{:S(2)}, u32[]{:S(2)}) %all-to-all-start.2) | async-done | bytes 2097184 | tf_op jit(solution)/shard_map/all_to_all | solution.py:15
  202.5 3.7 %fusion.5 = bf16[2,16,16,8,128]{4,3,2,1,0:T(8,128)(2,1)} fusion(bf16[2048,256,1]{1,0,2:T(8,128)(2,1)S(1)} %bitcast.65, bf16[32,2,64,256]{3,2,1,0:T(8,128)(2,1)S(1)} %all-to-all-done.2, bf16[64,32,128]{2,0,1:T(8,128)(2,1)} %copy-done.2, f32[128,256]{0,1:T(8,128)S(1)} %copy.12), kind=kOutput, calls=%fused_computation.6 | convolution fusion | flops 537526272 | bytes 4849664 | tf_op jit(solution)/shard_map/bq,npq->bnp/dot_general | solution.py:55
  206.2 1.5 copy.41
  207.7 56.5 %all_to_all.48 = bf16[16,128,2,128]{1,3,2,0:T(8,128)(2,1)S(1)} all-to-all(bf16[16,128,2,128]{1,3,2,0:T(8,128)(2,1)S(1)} %bitcast.66), channel_id=1, replica_groups=mesh['row'=32,'col'=16] {'col'}, dimensions={0} | all-to-all | bytes 2097152 | tf_op jit(solution)/shard_map/all_to_all | solution.py:30
  264.2 0.1 reduce_sum.12
  264.3 0.1 copy.19
  264.4 1.8 broadcast_in_dim.20
  266.3 0.0 copy-start.1
  266.3 5.8 %all-to-all-start.6 = ((bf16[32,128,2,128]{3,1,2,0:T(8,128)(2,1)}), bf16[32,128,2,128]{3,1,2,0:T(8,128)(2,1)S(1)}, u32[]{:S(2)}, u32[]{:S(2)}) async-start(bf16[32,128,2,128]{3,1,2,0:T(8,128)(2,1)} %broadcast_in_dim.20), calls=%async_computation.6 | async-start | bytes 4194304 | tf_op jit(solution)/shard_map/all_to_all | solution.py:15
  272.1 0.0 copy-done.1
  272.1 0.2 reshape.29
  272.4 49.6 %all-to-all-done.6 = bf16[32,128,2,128]{3,1,2,0:T(8,128)(2,1)S(1)} async-done(((bf16[32,128,2,128]{3,1,2,0:T(8,128)(2,1)}), bf16[32,128,2,128]{3,1,2,0:T(8,128)(2,1)S(1)}, u32[]{:S(2)}, u32[]{:S(2)}) %all-to-all-start.6) | async-done | bytes 2097184 | tf_op jit(solution)/shard_map/all_to_all | solution.py:15
  322.0 1.4 fusion.18
Async XLA Ops:
  0.0 76.1 %copy-start.3 = (bf16[64,256]{1,0:T(8,128)(2,1)S(1)}, bf16[64,256]{1,0:T(8,128)(2,1)}, u32[]{:S(2)}) copy-start(bf16[64,256]{1,0:T(8,128)(2,1)} %param.4) | copy-start | bytes 98308
  77.2 49.2 %all-to-all-start.1 = ((bf16[32,64,256]{2,1,0:T(8,128)(2,1)}), bf16[32,64,256]{2,1,0:T(8,128)(2,1)S(1)}, u32[]{:S(2)}, u32[]{:S(2)}) async-start(bf16[32,64,256]{2,1,0:T(8,128)(2,1)} %broadcast_in_dim.17), calls=%async_computation.1 | async-start | bytes 2097152 | tf_op jit(solution)/shard_map/all_to_all | solution.py:15
  98.9 31.7 %copy-start = (bf16[64,16,256]{2,1,0:T(8,128)(2,1)}, bf16[64,16,256]{2,1,0:T(8,128)(2,1)S(1)}, u32[]{:S(2)}) copy-start(bf16[64,16,256]{2,1,0:T(8,128)(2,1)S(1)} %copy.14) | copy-start | bytes 1572868
  126.4 20.7 %all-to-all-start.4 = ((bf16[64,32,128]{2,0,1:T(8,128)(2,1)}), bf16[64,32,128]{2,0,1:T(8,128)(2,1)S(1)}, u32[]{:S(2)}, u32[]{:S(2)}) async-start(bf16[64,32,128]{2,0,1:T(8,128)(2,1)} %copy.15), calls=%async_computation.4 | async-start | bytes 1048576 | tf_op jit(solution)/shard_map/all_to_all | solution.py:37
  147.1 1.6 copy-start.2
  148.7 3.9 %copy-start.4 = (f32[128,256]{1,0:T(8,128)S(1)}, f32[128,256]{1,0:T(8,128)}, u32[]{:S(2)}) copy-start(f32[128,256]{1,0:T(8,128)} %param.5) | copy-start | bytes 393220
  148.7 53.8 %all-to-all-start.2 = ((bf16[32,2,64,256]{3,2,1,0:T(8,128)(2,1)}), bf16[32,2,64,256]{3,2,1,0:T(8,128)(2,1)S(1)}, u32[]{:S(2)}, u32[]{:S(2)}) async-start(bf16[32,2,64,256]{3,2,1,0:T(8,128)(2,1)} %broadcast_in_dim.18), calls=%async_computation.2 | async-start | bytes 4194304 | tf_op jit(solution)/shard_map/all_to_all | solution.py:15
  266.3 5.8 %copy-start.1 = (bf16[64,16,256]{2,1,0:T(8,128)(2,1)S(1)}, bf16[64,16,256]{2,1,0:T(8,128)(2,1)}, u32[]{:S(2)}) copy-start(bf16[64,16,256]{2,1,0:T(8,128)(2,1)} %copy-done) | copy-start | bytes 1572868
  266.3 55.7 %all-to-all-start.6 = ((bf16[32,128,2,128]{3,1,2,0:T(8,128)(2,1)}), bf16[32,128,2,128]{3,1,2,0:T(8,128)(2,1)S(1)}, u32[]{:S(2)}, u32[]{:S(2)}) async-start(bf16[32,128,2,128]{3,1,2,0:T(8,128)(2,1)} %broadcast_in_dim.20), calls=%async_computation.6 | async-start | bytes 4194304 | tf_op jit(solution)/shard_map/all_to_all | solution.py:15
where the time goes:
time: 324 us; the launch traced here: 323 us
  waiting for transfers between devices  142 us (44%)
  blocking collectives  131 us (40%)
  starting transfers between devices  35 us (11%)
  local copies, waits for them, and re-layouts  9.69 us (3%)
  matrix products  5.35 us (2%)
    all_to_all x3, waiting for transfers between devices, sent_to_all(): return lax.all_to_all(copies, axis, split_axis=0, concat_axis=0, tiled=True)  126 us
    all_to_all x2, blocking collectives, sent_to_all(): return lax.all_to_all(copies, axis, split_axis=0, concat_axis=0, tiled=True)  74.4 us
    all_to_all x1, blocking collectives, sent_and_summed(): parts = lax.all_to_all(cut_along(value, dim, size), axis, 0, 0, tiled=True)  56.5 us
    all_to_all x3, starting transfers between devices, sent_to_all(): return lax.all_to_all(copies, axis, split_axis=0, concat_axis=0, tiled=True)  31.1 us
    all_to_all x1, waiting for transfers between devices, per_device(): lax.all_to_all(factor_rows, 'row', split_axis=1, concat_axis=0, tiled=True)  16.5 us
  transfers between devices with their start and end apart: 4, of which 4 were waited for; matrix products, arithmetic and copies ran while one was open for 1% of the time, Pallas kernels for 0%

commit v1 on v0

--- a/solution.py
+++ b/solution.py
@@ -34,7 +34,12 @@
 def per_device(amplitudes, factor, kernel):
     factor_cols = gathered_copies(factor, "row", 0)
     factor_rows = gathered_copies(factor, "col", 1)
-    factor_first = lax.all_to_all(factor_rows, "row", split_axis=1, concat_axis=0, tiled=True)
+    factor_first = jnp.concatenate(
+        lax.all_to_all(
+            jnp.stack(jnp.split(factor_rows, lax.axis_size("row"), axis=1)), "row", 0, 0
+        ),
+        axis=0,
+    )
     factor_part = factor_cols
     projected = jnp.einsum(
         "pak,kq->paq",

time: 324 us -> 325 us (level)
  blocking collectives: 131 us -> 102 us
  local copies, waits for them, and re-layouts: 9.69 us -> 28.6 us
  starting transfers between devices: 35 us -> 43.6 us
    all_to_all x2 -> x1, blocking collectives: 74.4 us -> 45.3 us  [sent_to_all(): return lax.all_to_all(copies, axis, split_axis=0, concat_axis=0, tiled=True)]
    unnamed x11 -> x42, local copies, waits for them, and re-layouts: 0.11 us -> 18.8 us
    all_to_all x3 -> x4, starting transfers between devices: 31.1 us -> 39.7 us  [sent_to_all(): return lax.all_to_all(copies, axis, split_axis=0, concat_axis=0, tiled=True)]
    all_to_all x3 -> x4, waiting for transfers between devices: 126 us -> 128 us  [sent_to_all(): return lax.all_to_all(copies, axis, split_axis=0, concat_axis=0, tiled=True)]
  transfers between devices with their start and end apart: 4 -> 5, of which waited for: 4 -> 5; matrix products, arithmetic and copies ran while one was open for 1% -> 6% of each run, Pallas kernels for 0% -> 0%
where the time goes in v1:
time: 325 us; the launch traced here: 324 us
  waiting for transfers between devices  145 us (45%)
  blocking collectives  102 us (31%)
  starting transfers between devices  43.6 us (13%)
  local copies, waits for them, and re-layouts  28.6 us (9%)
  matrix products  5.35 us (2%)
    all_to_all x4, waiting for transfers between devices, sent_to_all(): return lax.all_to_all(copies, axis, split_axis=0, concat_axis=0, tiled=True)  128 us
    all_to_all x1, blocking collectives, sent_and_summed(): parts = lax.all_to_all(cut_along(value, dim, size), axis, 0, 0, tiled=True)  56.5 us
    all_to_all x1, blocking collectives, sent_to_all(): return lax.all_to_all(copies, axis, split_axis=0, concat_axis=0, tiled=True)  45.3 us
    all_to_all x4, starting transfers between devices, sent_to_all(): return lax.all_to_all(copies, axis, split_axis=0, concat_axis=0, tiled=True)  39.7 us
    unnamed x42, local copies, waits for them, and re-layouts  18.8 us
    all_to_all x1, waiting for transfers between devices, per_device(): lax.all_to_all(jnp.stack(jnp.split(factor_rows, lax.axis_size('row'), axi...  16.5 us
    broadcast_in_dim x5, local copies, waits for them, and re-layouts, sent_to_all(): copies = jnp.broadcast_to(value, (lax.axis_size(axis), *value.shape))  7 us
  transfers between devices with their start and end apart: 5, of which 5 were waited for; matrix products, arithmetic and copies ran while one was open for 6% of the time, Pallas kernels for 0%

profile of v1, /device:TPU:1, one launch (start us, length us, event | category | flops | bytes accessed | tf_op | source)
XLA Modules:
  0.0 324.4 jit_solution(2200252400978301048)
XLA Ops:
  0.0 0.8 broadcast_in_dim.19
  0.8 0.0 copy-start.3
  0.8 45.3 %all_to_all.35 = bf16[16,64,256]{2,1,0:T(8,128)(2,1)S(1)} all-to-all(bf16[16,64,256]{2,1,0:T(8,128)(2,1)S(1)} %broadcast_in_dim.19), channel_id=1, replica_groups=mesh['row'=32,'col'=16] {'col'}, dimensions={0} | all-to-all | bytes 1048576 | tf_op jit(solution)/shard_map/all_to_all | solution.py:15
  46.1 1.7 broadcast_in_dim.16
  47.8 8.6 %all-to-all-start = ((bf16[16,2,64,128]{3,2,1,0:T(8,128)(2,1)}), bf16[16,2,64,128]{3,2,1,0:T(8,128)(2,1)S(1)}, u32[]{:S(2)}, u32[]{:S(2)}) async-start(bf16[16,2,64,128]{3,2,1,0:T(8,128)(2,1)} %broadcast_in_dim.16), calls=%async_computation | async-start | bytes 1048576 | tf_op jit(solution)/shard_map/all_to_all | solution.py:15
  56.5 0.6 constant_dynamic-update-slice_fusion.31
  57.1 0.6 constant_dynamic-update-slice_fusion.30
  57.7 0.6 constant_dynamic-update-slice_fusion.29
  58.3 0.6 constant_dynamic-update-slice_fusion.28
  58.9 0.6 constant_dynamic-update-slice_fusion.27
  59.5 0.6 constant_dynamic-update-slice_fusion.26
  60.1 0.6 constant_dynamic-update-slice_fusion.25
  60.7 0.6 constant_dynamic-update-slice_fusion.24
  61.3 0.6 constant_dynamic-update-slice_fusion.23
  61.9 0.6 constant_dynamic-update-slice_fusion.22
  62.5 0.6 constant_dynamic-update-slice_fusion.21
  63.1 0.6 constant_dynamic-update-slice_fusion.20
  63.7 0.6 constant_dynamic-update-slice_fusion.19
  64.3 12.8 %all-to-all-done = bf16[16,2,64,128]{3,2,1,0:T(8,128)(2,1)S(1)} async-done(((bf16[16,2,64,128]{3,2,1,0:T(8,128)(2,1)}), bf16[16,2,64,128]{3,2,1,0:T(8,128)(2,1)S(1)}, u32[]{:S(2)}, u32[]{:S(2)}) %all-to-all-start) | async-done | bytes 524320 | tf_op jit(solution)/shard_map/all_to_all | solution.py:15
  77.1 0.0 copy-done.3
  77.1 1.1 broadcast_in_dim.17
  78.2 0.0 copy-done
  78.2 21.4 %all-to-all-start.1 = ((bf16[32,64,256]{2,1,0:T(8,128)(2,1)}), bf16[32,64,256]{2,1,0:T(8,128)(2,1)S(1)}, u32[]{:S(2)}, u32[]{:S(2)}) async-start(bf16[32,64,256]{2,1,0:T(8,128)(2,1)} %broadcast_in_dim.17), calls=%async_computation.1 | async-start | bytes 2097152 | tf_op jit(solution)/shard_map/all_to_all | solution.py:15
  99.6 0.6 constant_dynamic-update-slice_fusion.18
  100.2 0.6 constant_dynamic-update-slice_fusion.17
  100.8 0.6 constant_dynamic-update-slice_fusion.16
  101.4 0.6 constant_dynamic-update-slice_fusion.15
  102.0 0.6 constant_dynamic-update-slice_fusion.14
  102.6 0.6 constant_dynamic-update-slice_fusion.13
  103.3 0.6 constant_dynamic-update-slice_fusion.12
  103.9 0.6 constant_dynamic-update-slice_fusion.11
  104.5 0.6 constant_dynamic-update-slice_fusion.10
  105.1 0.6 constant_dynamic-update-slice_fusion.9
  105.7 0.6 constant_dynamic-update-slice_fusion.8
  106.3 0.6 constant_dynamic-update-slice_fusion.7
  106.9 0.6 constant_dynamic-update-slice_fusion.6
  107.5 0.6 constant_dynamic-update-slice_fusion.5
  108.1 0.6 constant_dynamic-update-slice_fusion.4
  108.7 0.6 constant_dynamic-update-slice_fusion.3
  109.3 0.6 constant_dynamic-update-slice_fusion.2
  109.9 0.6 constant_dynamic-update-slice_fusion.1
  110.5 0.6 constant_dynamic-update-slice_fusion
  111.1 16.4 %all-to-all-done.1 = bf16[32,64,256]{2,1,0:T(8,128)(2,1)S(1)} async-done(((bf16[32,64,256]{2,1,0:T(8,128)(2,1)}), bf16[32,64,256]{2,1,0:T(8,128)(2,1)S(1)}, u32[]{:S(2)}, u32[]{:S(2)}) %all-to-all-start.1) | async-done | bytes 1048608 | tf_op jit(solution)/shard_map/all_to_all | solution.py:15
  127.5 3.9 %all-to-all-start.4 = ((bf16[32,64,128]{2,1,0:T(8,128)(2,1)}), bf16[32,64,128]{2,1,0:T(8,128)(2,1)S(1)}, u32[]{:S(2)}, u32[]{:S(2)}) async-start(bf16[32,64,128]{2,1,0:T(8,128)(2,1)} %constant_dynamic-update-slice_fusion), calls=%async_computation.4 | async-start | bytes 1048576 | tf_op jit(solution)/shard_map/all_to_all | solution.py:38
  131.3 0.3 convolution_convert_fusion.1
  131.6 16.5 %all-to-all-done.4 = bf16[32,64,128]{2,1,0:T(8,128)(2,1)S(1)} async-done(((bf16[32,64,128]{2,1,0:T(8,128)(2,1)}), bf16[32,64,128]{2,1,0:T(8,128)(2,1)S(1)}, u32[]{:S(2)}, u32[]{:S(2)}) %all-to-all-start.4) | async-done | bytes 524320 | tf_op jit(solution)/shard_map/all_to_all | solution.py:38
  148.1 1.6 broadcast_in_dim.18
  149.7 0.0 copy-done.2
  149.7 3.9 %all-to-all-start.2 = ((bf16[32,2,64,256]{3,2,1,0:T(8,128)(2,1)}), bf16[32,2,64,256]{3,2,1,0:T(8,128)(2,1)S(1)}, u32[]{:S(2)}, u32[]{:S(2)}) async-start(bf16[32,2,64,256]{3,2,1,0:T(8,128)(2,1)} %broadcast_in_dim.18), calls=%async_computation.2 | async-start | bytes 4194304 | tf_op jit(solution)/shard_map/all_to_all | solution.py:15
  153.7 0.0 copy-done.4
  153.7 0.1 copy.4
  153.8 49.8 %all-to-all-done.2 = bf16[32,2,64,256]{3,2,1,0:T(8,128)(2,1)S(1)} async-done(((bf16[32,2,64,256]{3,2,1,0:T(8,128)(2,1)}), bf16[32,2,64,256]{3,2,1,0:T(8,128)(2,1)S(1)}, u32[]{:S(2)}, u32[]{:S(2)}) %all-to-all-start.2) | async-done | bytes 2097184 | tf_op jit(solution)/shard_map/all_to_all | solution.py:15
  203.5 3.7 %fusion.5 = bf16[2,16,16,8,128]{4,3,2,1,0:T(8,128)(2,1)} fusion(bf16[2048,256,1]{1,0,2:T(8,128)(2,1)S(1)} %bitcast.193, bf16[32,2,64,256]{3,2,1,0:T(8,128)(2,1)S(1)} %all-to-all-done.2, bf16[32,64,128]{2,1,0:T(8,128)(2,1)} %copy-done.2, f32[128,256]{0,1:T(8,128)S(1)} %copy.4), kind=kOutput, calls=%fused_computation.6 | convolution fusion | flops 537526272 | bytes 4849664 | tf_op jit(solution)/shard_map/bq,npq->bnp/dot_general | solution.py:60
  207.2 1.5 copy.32
  208.7 56.5 %all_to_all.36 = bf16[16,128,2,128]{1,3,2,0:T(8,128)(2,1)S(1)} all-to-all(bf16[16,128,2,128]{1,3,2,0:T(8,128)(2,1)S(1)} %bitcast.196), channel_id=1, replica_groups=mesh['row'=32,'col'=16] {'col'}, dimensions={0} | all-to-all | bytes 2097152 | tf_op jit(solution)/shard_map/all_to_all | solution.py:30
  265.2 0.1 reduce_sum.12
  265.3 0.1 copy.10
  265.5 1.8 broadcast_in_dim.20
  267.3 5.8 %all-to-all-start.6 = ((bf16[32,128,2,128]{3,1,2,0:T(8,128)(2,1)}), bf16[32,128,2,128]{3,1,2,0:T(8,128)(2,1)S(1)}, u32[]{:S(2)}, u32[]{:S(2)}) async-start(bf16[32,128,2,128]{3,1,2,0:T(8,128)(2,1)} %broadcast_in_dim.20), calls=%async_computation.6 | async-start | bytes 4194304 | tf_op jit(solution)/shard_map/all_to_all | solution.py:15
  273.1 0.0 copy-done.1
  273.1 0.3 copy.6
  273.4 0.2 reshape.26
  273.7 49.3 %all-to-all-done.6 = bf16[32,128,2,128]{3,1,2,0:T(8,128)(2,1)S(1)} async-done(((bf16[32,128,2,128]{3,1,2,0:T(8,128)(2,1)}), bf16[32,128,2,128]{3,1,2,0:T(8,128)(2,1)S(1)}, u32[]{:S(2)}, u32[]{:S(2)}) %all-to-all-start.6) | async-done | bytes 2097184 | tf_op jit(solution)/shard_map/all_to_all | solution.py:15
  323.0 1.4 fusion.18
  (5 shorter events, 0.0 us)
Async XLA Ops:
  0.8 76.3 %copy-start.3 = (bf16[64,256]{1,0:T(8,128)(2,1)S(1)}, bf16[64,256]{1,0:T(8,128)(2,1)}, u32[]{:S(2)}) copy-start(bf16[64,256]{1,0:T(8,128)(2,1)} %param.4) | copy-start | bytes 98308
  46.1 32.1 %copy-start = (bf16[16,64,256]{2,1,0:T(8,128)(2,1)}, bf16[16,64,256]{2,1,0:T(8,128)(2,1)S(1)}, u32[]{:S(2)}) copy-start(bf16[16,64,256]{2,1,0:T(8,128)(2,1)S(1)} %all_to_all.35) | copy-start | bytes 1572868
  47.8 29.3 %all-to-all-start = ((bf16[16,2,64,128]{3,2,1,0:T(8,128)(2,1)}), bf16[16,2,64,128]{3,2,1,0:T(8,128)(2,1)S(1)}, u32[]{:S(2)}, u32[]{:S(2)}) async-start(bf16[16,2,64,128]{3,2,1,0:T(8,128)(2,1)} %broadcast_in_dim.16), calls=%async_computation | async-start | bytes 1048576 | tf_op jit(solution)/shard_map/all_to_all | solution.py:15
  78.2 49.2 %all-to-all-start.1 = ((bf16[32,64,256]{2,1,0:T(8,128)(2,1)}), bf16[32,64,256]{2,1,0:T(8,128)(2,1)S(1)}, u32[]{:S(2)}, u32[]{:S(2)}) async-start(bf16[32,64,256]{2,1,0:T(8,128)(2,1)} %broadcast_in_dim.17), calls=%async_computation.1 | async-start | bytes 2097152 | tf_op jit(solution)/shard_map/all_to_all | solution.py:15
  127.5 20.7 %all-to-all-start.4 = ((bf16[32,64,128]{2,1,0:T(8,128)(2,1)}), bf16[32,64,128]{2,1,0:T(8,128)(2,1)S(1)}, u32[]{:S(2)}, u32[]{:S(2)}) async-start(bf16[32,64,128]{2,1,0:T(8,128)(2,1)} %constant_dynamic-update-slice_fusion), calls=%async_computation.4 | async-start | bytes 1048576 | tf_op jit(solution)/shard_map/all_to_all | solution.py:38
  148.1 1.6 copy-start.2
  149.7 3.9 %copy-start.4 = (f32[128,256]{1,0:T(8,128)S(1)}, f32[128,256]{1,0:T(8,128)}, u32[]{:S(2)}) copy-start(f32[128,256]{1,0:T(8,128)} %param.5) | copy-start | bytes 393220
  149.7 53.8 %all-to-all-start.2 = ((bf16[32,2,64,256]{3,2,1,0:T(8,128)(2,1)}), bf16[32,2,64,256]{3,2,1,0:T(8,128)(2,1)S(1)}, u32[]{:S(2)}, u32[]{:S(2)}) async-start(bf16[32,2,64,256]{3,2,1,0:T(8,128)(2,1)} %broadcast_in_dim.18), calls=%async_computation.2 | async-start | bytes 4194304 | tf_op jit(solution)/shard_map/all_to_all | solution.py:15
  267.3 5.8 %copy-start.1 = (bf16[16,64,256]{2,1,0:T(8,128)(2,1)S(1)}, bf16[16,64,256]{2,1,0:T(8,128)(2,1)}, u32[]{:S(2)}) copy-start(bf16[16,64,256]{2,1,0:T(8,128)(2,1)} %copy-done) | copy-start | bytes 1572868
  267.3 55.7 %all-to-all-start.6 = ((bf16[32,128,2,128]{3,1,2,0:T(8,128)(2,1)}), bf16[32,128,2,128]{3,1,2,0:T(8,128)(2,1)S(1)}, u32[]{:S(2)}, u32[]{:S(2)}) async-start(bf16[32,128,2,128]{3,1,2,0:T(8,128)(2,1)} %broadcast_in_dim.20), calls=%async_computation.6 | async-start | bytes 4194304 | tf_op jit(solution)/shard_map/all_to_all | solution.py:15
